TPU v7x, 32 devices: a whole 2x2x4 slice. The times are simulated.
32 devices in a mesh: gx: 8 (over y, x, core), gz: 4 (over z).
Axes of the slice: x: 2, y: 2, z: 4, core: 2. Of those that a mesh axis runs over, the one named last changes fastest.
Arguments:
- velocity_old: float32 [3, 64, 64, 128], P(None, 'gx', 'gz'), may hold values from -6 to 6
- source: float32 [3, 64, 64, 128], P(None, 'gx', 'gz'), may hold values from -6 to 6
- diag_coef: float32 [64, 64, 128], P('gx', 'gz'), may hold values from 0.5 to 2
- face_coef: float32 [3, 64, 64, 128], P(None, 'gx', 'gz'), may hold values from 0.2 to 2
- bc_flags: int32 [2, 64, 64], P(None, 'gx', 'gz'), may hold values from 0 to 1
- coarse_map: int32 [64, 64, 128], P('gx', 'gz'), may hold values from 0 to 15
- coarse_inverse: float32 [512, 64], P('gx'), may hold values from -0.1 to 0.3
Outputs:
- velocity: float32 [3, 64, 64, 128], P(None, 'gx', 'gz')
- pressure: float32 [64, 64, 128], P('gx', 'gz')
All inputs are finite; a program needn't handle non-finite values.
Results may differ from a plain program's by a relative error of at most 0.0003.
Values sent between devices are 32-bit elements; how exact they have to be, the bound alone decides.
A program may use at most 64 MiB of HBM per device.

v0:
```python
import jax
import jax.numpy as jnp
from jax import lax
from jax.sharding import PartitionSpec as P

COARSE = 16
jacobi_weight = 2.0 / 3.0


def passed_along(value, axis, steps):
    count = lax.axis_size(axis)
    pairs = [(source, (source + steps) % count) for source in range(count)]
    return lax.ppermute(value, axis, pairs)


def with_halo(array, sides, width):
    for axis, dim in sides:
        count, length = (lax.axis_size(axis), array.shape[dim])
        up = [(i, (i + 1) % count) for i in range(count)]
        down = [(j, i) for i, j in up]
        last = lax.slice_in_dim(array, length - width, length, axis=dim)
        initial = lax.slice_in_dim(array, 0, width, axis=dim)
        before = lax.ppermute(last, axis, up)
        after = lax.ppermute(initial, axis, down)
        array = jnp.concatenate([before, array, after], axis=dim)
    return array


def inner_local(left, right):
    return jnp.sum(left * right, axis=(1, 2, 3))


def widen(value):
    return value[:, None, None, None]


def global_sums(pairs):
    local = jnp.stack([inner_local(left, right) for left, right in pairs])
    return lax.psum(local, ("gx", "gz"))


def solve_values(velocity_old, source, diag_coef, face_coef):
    coef_x, coef_z, coef_y = (face_coef[0], face_coef[1], face_coef[2])
    count_y = coef_y.shape[-1]
    level = lax.broadcasted_iota(jnp.int32, coef_y.shape, 2)
    wall = jnp.where((level == 0) | (level == count_y - 1), coef_y[..., -1:], 0.0)
    west_cx = passed_along(coef_x[-1:], "gx", 1)
    south_cz = passed_along(coef_z[:, -1:], "gz", 1)
    wide_cx = jnp.concatenate([west_cx, coef_x], 0)
    wide_cz = jnp.concatenate([south_cz, coef_z], 1)

    def apply(field):
        padded = with_halo(field, (("gx", 1), ("gz", 2)), 1)
        flux_x = wide_cx * (padded[:, :-1, 1:-1] - padded[:, 1:, 1:-1])
        flux_z = wide_cz * (padded[:, 1:-1, :-1] - padded[:, 1:-1, 1:])
        planar = flux_x[:, 1:] - flux_x[:, :-1] + (flux_z[:, :, 1:] - flux_z[:, :, :-1])
        grad_y = coef_y[..., :-1] * (field[..., :-1] - field[..., 1:])
        zero = jnp.zeros_like(field[..., :1])
        vertical = (
            jnp.concatenate([grad_y, zero], -1) - jnp.concatenate([zero, grad_y], -1) + wall * field
        )
        return diag_coef * field + planar + vertical

    x = velocity_old
    r = source - apply(x)
    r0 = r
    p = r
    v = apply(p)
    first = global_sums([(r0, r0), (r0, v)])
    rho = first[0]
    alpha = rho / first[1]
    s = r - widen(alpha) * v
    t = apply(s)
    second = global_sums([(t, s), (t, t), (r0, s), (r0, t)])
    omega = second[0] / second[1]
    x = x + widen(alpha) * p + widen(omega) * s
    r = s - widen(omega) * t
    rho_new = second[2] - omega * second[3]
    beta = rho_new / rho * (alpha / omega)
    p = r + widen(beta) * (p - widen(omega) * v)
    v = apply(p)
    third = global_sums([(r0, v)])
    alpha = rho_new / third[0]
    s = r - widen(alpha) * v
    t = apply(s)
    fourth = global_sums([(t, s), (t, t)])
    omega = fourth[0] / fourth[1]
    return x + widen(alpha) * p + widen(omega) * s


def body(velocity_old, source, diag_coef, face_coef, bc_flags, coarse_map, coarse_inverse):
    coef_y = face_coef[2]
    count_y = coef_y.shape[-1]
    level = lax.broadcasted_iota(jnp.int32, coef_y.shape, 2)
    velocity = solve_values(velocity_old, source, diag_coef, face_coef)
    along_x, along_z, along_y = (velocity[0], velocity[1], velocity[2])
    west_u = passed_along(along_x[-1:], "gx", 1)
    south_w = passed_along(along_z[:, -1:], "gz", 1)
    zero = jnp.zeros_like(along_y[..., :1])
    div = (
        along_x
        - jnp.concatenate([west_u, along_x[:-1]], 0)
        + (along_z - jnp.concatenate([south_w, along_z[:, :-1]], 1))
    )
    div = div + (along_y - jnp.concatenate([zero, along_y[..., :-1]], -1))
    flags = bc_flags.astype(jnp.float32)
    bottom = level == 0
    top = level == count_y - 1
    pdiag = 6.0 - bottom.astype(jnp.float32) - top.astype(jnp.float32)
    pdiag = (
        pdiag
        + jnp.where(bottom, flags[0][..., None], 0.0)
        + jnp.where(top, flags[1][..., None], 0.0)
    )

    def pressure_apply(field):
        padded = with_halo(field, (("gx", 0), ("gz", 1)), 1)
        beside = padded[2:, 1:-1] + padded[:-2, 1:-1] + (padded[1:-1, 2:] + padded[1:-1, :-2])
        beside = beside + (
            jnp.concatenate([field[..., 1:], zero], -1)
            + jnp.concatenate([zero, field[..., :-1]], -1)
        )
        return pdiag * field - beside

    q = jacobi_weight * div / pdiag
    q = q + jacobi_weight * (div - pressure_apply(q)) / pdiag
    res = div - pressure_apply(q)
    labels = lax.broadcasted_iota(jnp.int32, (COARSE, 1, 1, 1), 0)
    onehot = (coarse_map[None] == labels).astype(jnp.float32)
    coarse = jnp.einsum("kxzy,xzy->k", onehot, res, precision=lax.Precision.HIGHEST)
    offset = lax.axis_index("gz") * COARSE
    columns = lax.dynamic_slice_in_dim(coarse_inverse, offset, COARSE, 1)
    own = lax.psum_scatter(
        jnp.dot(columns, coarse, precision=lax.Precision.HIGHEST),
        "gz",
        scatter_dimension=0,
        tiled=True,
    )
    q = q + jnp.einsum("kxzy,k->xzy", onehot, own, precision=lax.Precision.HIGHEST)
    for sweep in range(2):
        q = q + jacobi_weight * (div - pressure_apply(q)) / pdiag
    return (velocity, q)


def solution(mesh):
    placed = (
        P(None, "gx", "gz", None),
        P(None, "gx", "gz", None),
        P("gx", "gz", None),
        P(None, "gx", "gz", None),
        P(None, "gx", "gz"),
        P("gx", "gz", None),
        P("gx", None),
    )
    return jax.shard_map(
        body,
        mesh=mesh,
        in_specs=placed,
        out_specs=(P(None, "gx", "gz", None), P("gx", "gz", None)),
        check_vma=False,
    )
```

profile of v0, /device:TPU:0, one launch (start us, length us, event | category | flops | bytes accessed | tf_op | source)
XLA Modules:
  0.0 278.5 jit_solution(2390331848632894776)
XLA Ops:
  1.6 3.1 %collective-permute-start.3 = (f32[8,1,128]{2,1,0:T(1,128)S(1)}, f32[8,1,128]{2,1,0:T(1,128)S(1)}, u32[]{:S(2)}, u32[]{:S(2)}) collective-permute-start(f32[8,1,128]{2,1,0:T(1,128)S(1)} %slice.567), channel_id=1, source_target_pairs={{0,1},{1,2},{2,3},{3,0},{4,5},{5,6},{6,7},{7,4},{8,9},{9,10},{10,1... | collective-permute-start | bytes 12296 | tf_op jit(solution)/shard_map/ppermute | solution.py:13
  4.8 2.6 collective-permute-start.2
  9.5 2.6 collective-permute-done
  13.8 2.2 collective-permute-start.5
  18.1 2.6 collective-permute-start.7
  23.9 2.5 collective-permute-start.9
  28.4 39.4 %psum.28 = f32[2,3]{1,0:T(2,128)S(1)} all-reduce(f32[2,3]{1,0:T(2,128)S(1)} %pad_maximum_fusion.85), channel_id=1, replica_groups=mesh['gx'=8,'gz'=4] {'gx','gz'}, use_global_device_ids=true, to_apply=%region_2.3 | all-reduce | flops 6 | bytes 48 | tf_op jit(solution)/shard_map/psum | solution.py:39
  68.0 2.6 collective-permute-start.11
  72.2 1.9 collective-permute-start.12
  74.1 2.0 collective-permute-start.13
  78.3 39.7 %psum.29 = f32[4,3]{1,0:T(4,128)S(1)} all-reduce(f32[4,3]{1,0:T(4,128)S(1)} %pad_maximum_fusion.84), channel_id=1, replica_groups=mesh['gx'=8,'gz'=4] {'gx','gz'}, use_global_device_ids=true, to_apply=%region_7.8 | all-reduce | flops 12 | bytes 96 | tf_op jit(solution)/shard_map/psum | solution.py:39
  118.2 2.6 collective-permute-start.15
  122.4 2.1 collective-permute-start.16
  128.5 40.0 %psum.30 = f32[3]{0:T(128)S(1)} all-reduce(f32[3]{0:T(128)S(1)} %get-tuple-element.12), channel_id=1, replica_groups=mesh['gx'=8,'gz'=4] {'gx','gz'}, use_global_device_ids=true, to_apply=%region_9.10 | all-reduce | flops 3 | bytes 24 | tf_op jit(solution)/shard_map/psum | solution.py:39
  168.7 2.6 collective-permute-start.19
  172.9 1.9 collective-permute-start.20
  174.8 2.0 collective-permute-start.21
  179.0 39.7 %psum.31 = f32[2,3]{1,0:T(2,128)S(1)} all-reduce(f32[2,3]{1,0:T(2,128)S(1)} %pad_maximum_fusion.86), channel_id=1, replica_groups=mesh['gx'=8,'gz'=4] {'gx','gz'}, use_global_device_ids=true, to_apply=%region_12.13 | all-reduce | flops 6 | bytes 48 | tf_op jit(solution)/shard_map/psum | solution.py:39
  218.9 2.1 collective-permute-start.23
  221.0 3.3 %collective-permute-done.23 = f32[8,1,128]{2,1,0:T(1,128)S(1)} collective-permute-done((f32[8,1,128]{2,1,0:T(1,128)S(1)}, f32[8,1,128]{2,1,0:T(1,128)S(1)}, u32[]{:S(2)}, u32[]{:S(2)}) %collective-permute-start.23) | collective-permute-done | bytes 4128 | tf_op jit(solution)/shard_map/ppermute | solution.py:13
  226.6 2.6 collective-permute-done.25
  229.3 1.8 collective-permute-start.26
  232.9 3.5 %collective-permute-done.27 = f32[10,1,128]{2,1,0:T(1,128)S(1)} collective-permute-done((f32[10,1,128]{2,1,0:T(1,128)S(1)}, f32[10,1,128]{2,1,0:T(1,128)S(1)}, u32[]{:S(2)}, u32[]{:S(2)}) %collective-permute-start.27) | collective-permute-done | bytes 5152 | tf_op jit(solution)/shard_map/ppermute | solution.py:23
  240.8 2.0 collective-permute-start.31
  244.4 1.9 collective-permute-done.31
  247.4 8.5 %all-reduce.19 = f32[64]{0:T(128)S(1)} all-reduce(f32[64]{0:T(128)S(1)} %convolution_bitcast_fusion), channel_id=2, replica_groups=mesh['gx'=8,'gz'=4] {'gz'}, use_global_device_ids=true, to_apply=%region_13.14.clone | all-reduce | flops 64 | bytes 512
  257.9 2.7 collective-permute-done.33
  260.6 1.9 collective-permute-start.34
  264.3 3.7 %collective-permute-done.35 = f32[10,1,128]{2,1,0:T(1,128)S(1)} collective-permute-done((f32[10,1,128]{2,1,0:T(1,128)S(1)}, f32[10,1,128]{2,1,0:T(1,128)S(1)}, u32[]{:S(2)}, u32[]{:S(2)}) %collective-permute-start.35) | collective-permute-done | bytes 5152 | tf_op jit(solution)/shard_map/ppermute | solution.py:23
  269.5 2.7 collective-permute-done.37
  272.2 2.0 collective-permute-start.39
  275.8 1.9 collective-permute-done.39
  (155 shorter events, 43.8 us)
Async XLA Ops:
  1.6 7.8 %collective-permute-start.3 = (f32[8,1,128]{2,1,0:T(1,128)S(1)}, f32[8,1,128]{2,1,0:T(1,128)S(1)}, u32[]{:S(2)}, u32[]{:S(2)}) collective-permute-start(f32[8,1,128]{2,1,0:T(1,128)S(1)} %slice.567), channel_id=1, source_target_pairs={{0,1},{1,2},{2,3},{3,0},{4,5},{5,6},{6,7},{7,4},{8,9},{9,10},{10,1... | collective-permute-start | bytes 12296 | tf_op jit(solution)/shard_map/ppermute | solution.py:13
  4.7 7.3 %collective-permute-start.1 = (f32[3,1,16,128]{3,2,1,0:T(8,128)S(1)}, f32[3,1,16,128]{3,2,1,0:T(8,128)S(1)}, u32[]{:S(2)}, u32[]{:S(2)}) collective-permute-start(f32[3,1,16,128]{3,2,1,0:T(8,128)S(1)} %get-tuple-element.42), channel_id=1, source_target_pairs={{0,4},{4,8},{8,12},{12,16},{16,20},{20,24},{24,28},{28,0},{1,5},{5... | collective-permute-start | bytes 73736 | tf_op jit(solution)/shard_map/ppermute | solution.py:23
  4.8 7.4 %collective-permute-start.2 = (f32[3,1,16,128]{3,2,1,0:T(8,128)S(1)}, f32[3,1,16,128]{3,2,1,0:T(8,128)S(1)}, u32[]{:S(2)}, u32[]{:S(2)}) collective-permute-start(f32[3,1,16,128]{3,2,1,0:T(8,128)S(1)} %get-tuple-element.41), channel_id=1, source_target_pairs={{4,0},{8,4},{12,8},{16,12},{20,16},{24,20},{28,24},{0,28},{5,1},{9... | collective-permute-start | bytes 73736 | tf_op jit(solution)/shard_map/ppermute | solution.py:24
  8.1 4.0 %collective-permute-start = (f32[1,16,128]{2,1,0:T(8,128)S(1)}, f32[1,16,128]{2,1,0:T(8,128)S(1)}, u32[]{:S(2)}, u32[]{:S(2)}) collective-permute-start(f32[1,16,128]{2,1,0:T(8,128)S(1)} %slice_bitcast_fusion.7), channel_id=1, source_target_pairs={{0,4},{4,8},{8,12},{12,16},{16,20},{20,24},{24,28},{28,0},{1,5},{5... | collective-permute-start | bytes 24584 | tf_op jit(solution)/shard_map/ppermute | solution.py:13
  12.2 5.6 %collective-permute-start.4 = (f32[3,10,1,128]{3,2,1,0:T(1,128)S(1)}, f32[3,10,1,128]{3,2,1,0:T(1,128)S(1)}, u32[]{:S(2)}, u32[]{:S(2)}) collective-permute-start(f32[3,10,1,128]{3,2,1,0:T(1,128)S(1)} %get-tuple-element.26), channel_id=1, source_target_pairs={{0,1},{1,2},{2,3},{3,0},{4,5},{5,6},{6,7},{7,4},{8,9},{9,10},{10,1... | collective-permute-start | bytes 46088 | tf_op jit(solution)/shard_map/ppermute | solution.py:23
  13.8 4.0 %collective-permute-start.5 = (f32[3,10,1,128]{3,2,1,0:T(1,128)S(1)}, f32[3,10,1,128]{3,2,1,0:T(1,128)S(1)}, u32[]{:S(2)}, u32[]{:S(2)}) collective-permute-start(f32[3,10,1,128]{3,2,1,0:T(1,128)S(1)} %get-tuple-element.27), channel_id=1, source_target_pairs={{1,0},{2,1},{3,2},{0,3},{5,4},{6,5},{7,6},{4,7},{9,8},{10,9},{11,1... | collective-permute-start | bytes 46088 | tf_op jit(solution)/shard_map/ppermute | solution.py:24
  18.0 4.4 %collective-permute-start.6 = (f32[3,1,16,128]{3,2,1,0:T(8,128)S(1)}, f32[3,1,16,128]{3,2,1,0:T(8,128)S(1)}, u32[]{:S(2)}, u32[]{:S(2)}) collective-permute-start(f32[3,1,16,128]{3,2,1,0:T(8,128)S(1)} %get-tuple-element.36), channel_id=1, source_target_pairs={{0,4},{4,8},{8,12},{12,16},{16,20},{20,24},{24,28},{28,0},{1,5},{5... | collective-permute-start | bytes 73736 | tf_op jit(solution)/shard_map/ppermute | solution.py:23
  18.1 4.4 %collective-permute-start.7 = (f32[3,1,16,128]{3,2,1,0:T(8,128)S(1)}, f32[3,1,16,128]{3,2,1,0:T(8,128)S(1)}, u32[]{:S(2)}, u32[]{:S(2)}) collective-permute-start(f32[3,1,16,128]{3,2,1,0:T(8,128)S(1)} %get-tuple-element.37), channel_id=1, source_target_pairs={{4,0},{8,4},{12,8},{16,12},{20,16},{24,20},{28,24},{0,28},{5,1},{9... | collective-permute-start | bytes 73736 | tf_op jit(solution)/shard_map/ppermute | solution.py:24
  22.5 5.6 %collective-permute-start.8 = (f32[3,10,1,128]{3,2,1,0:T(1,128)S(1)}, f32[3,10,1,128]{3,2,1,0:T(1,128)S(1)}, u32[]{:S(2)}, u32[]{:S(2)}) collective-permute-start(f32[3,10,1,128]{3,2,1,0:T(1,128)S(1)} %get-tuple-element.24), channel_id=1, source_target_pairs={{0,1},{1,2},{2,3},{3,0},{4,5},{5,6},{6,7},{7,4},{8,9},{9,10},{10,1... | collective-permute-start | bytes 46088 | tf_op jit(solution)/shard_map/ppermute | solution.py:23
  23.9 4.2 %collective-permute-start.9 = (f32[3,10,1,128]{3,2,1,0:T(1,128)S(1)}, f32[3,10,1,128]{3,2,1,0:T(1,128)S(1)}, u32[]{:S(2)}, u32[]{:S(2)}) collective-permute-start(f32[3,10,1,128]{3,2,1,0:T(1,128)S(1)} %get-tuple-element.25), channel_id=1, source_target_pairs={{1,0},{2,1},{3,2},{0,3},{5,4},{6,5},{7,6},{4,7},{9,8},{10,9},{11,1... | collective-permute-start | bytes 46088 | tf_op jit(solution)/shard_map/ppermute | solution.py:24
  67.9 4.2 %collective-permute-start.10 = (f32[3,1,16,128]{3,2,1,0:T(8,128)S(1)}, f32[3,1,16,128]{3,2,1,0:T(8,128)S(1)}, u32[]{:S(2)}, u32[]{:S(2)}) collective-permute-start(f32[3,1,16,128]{3,2,1,0:T(8,128)S(1)} %get-tuple-element.34), channel_id=1, source_target_pairs={{0,4},{4,8},{8,12},{12,16},{16,20},{20,24},{24,28},{28,0},{1,5},{5... | collective-permute-start | bytes 73736 | tf_op jit(solution)/shard_map/ppermute | solution.py:23
  68.0 4.2 %collective-permute-start.11 = (f32[3,1,16,128]{3,2,1,0:T(8,128)S(1)}, f32[3,1,16,128]{3,2,1,0:T(8,128)S(1)}, u32[]{:S(2)}, u32[]{:S(2)}) collective-permute-start(f32[3,1,16,128]{3,2,1,0:T(8,128)S(1)} %get-tuple-element.35), channel_id=1, source_target_pairs={{4,0},{8,4},{12,8},{16,12},{20,16},{24,20},{28,24},{0,28},{5,1},{9... | collective-permute-start | bytes 73736 | tf_op jit(solution)/shard_map/ppermute | solution.py:24
  72.2 5.6 %collective-permute-start.12 = (f32[3,10,1,128]{3,2,1,0:T(1,128)S(1)}, f32[3,10,1,128]{3,2,1,0:T(1,128)S(1)}, u32[]{:S(2)}, u32[]{:S(2)}) collective-permute-start(f32[3,10,1,128]{3,2,1,0:T(1,128)S(1)} %get-tuple-element.22), channel_id=1, source_target_pairs={{0,1},{1,2},{2,3},{3,0},{4,5},{5,6},{6,7},{7,4},{8,9},{9,10},{10,1... | collective-permute-start | bytes 46088 | tf_op jit(solution)/shard_map/ppermute | solution.py:23
  74.1 3.9 %collective-permute-start.13 = (f32[3,10,1,128]{3,2,1,0:T(1,128)S(1)}, f32[3,10,1,128]{3,2,1,0:T(1,128)S(1)}, u32[]{:S(2)}, u32[]{:S(2)}) collective-permute-start(f32[3,10,1,128]{3,2,1,0:T(1,128)S(1)} %get-tuple-element.23), channel_id=1, source_target_pairs={{1,0},{2,1},{3,2},{0,3},{5,4},{6,5},{7,6},{4,7},{9,8},{10,9},{11,1... | collective-permute-start | bytes 46088 | tf_op jit(solution)/shard_map/ppermute | solution.py:24
  118.1 4.2 %collective-permute-start.14 = (f32[3,1,16,128]{3,2,1,0:T(8,128)S(1)}, f32[3,1,16,128]{3,2,1,0:T(8,128)S(1)}, u32[]{:S(2)}, u32[]{:S(2)}) collective-permute-start(f32[3,1,16,128]{3,2,1,0:T(8,128)S(1)} %get-tuple-element.32), channel_id=1, source_target_pairs={{0,4},{4,8},{8,12},{12,16},{16,20},{20,24},{24,28},{28,0},{1,5},{5... | collective-permute-start | bytes 73736 | tf_op jit(solution)/shard_map/ppermute | solution.py:23
  118.2 4.2 %collective-permute-start.15 = (f32[3,1,16,128]{3,2,1,0:T(8,128)S(1)}, f32[3,1,16,128]{3,2,1,0:T(8,128)S(1)}, u32[]{:S(2)}, u32[]{:S(2)}) collective-permute-start(f32[3,1,16,128]{3,2,1,0:T(8,128)S(1)} %get-tuple-element.33), channel_id=1, source_target_pairs={{4,0},{8,4},{12,8},{16,12},{20,16},{24,20},{28,24},{0,28},{5,1},{9... | collective-permute-start | bytes 73736 | tf_op jit(solution)/shard_map/ppermute | solution.py:24
  122.4 5.6 %collective-permute-start.16 = (f32[3,10,1,128]{3,2,1,0:T(1,128)S(1)}, f32[3,10,1,128]{3,2,1,0:T(1,128)S(1)}, u32[]{:S(2)}, u32[]{:S(2)}) collective-permute-start(f32[3,10,1,128]{3,2,1,0:T(1,128)S(1)} %get-tuple-element.20), channel_id=1, source_target_pairs={{0,1},{1,2},{2,3},{3,0},{4,5},{5,6},{6,7},{7,4},{8,9},{9,10},{10,1... | collective-permute-start | bytes 46088 | tf_op jit(solution)/shard_map/ppermute | solution.py:23
  124.5 3.7 %collective-permute-start.17 = (f32[3,10,1,128]{3,2,1,0:T(1,128)S(1)}, f32[3,10,1,128]{3,2,1,0:T(1,128)S(1)}, u32[]{:S(2)}, u32[]{:S(2)}) collective-permute-start(f32[3,10,1,128]{3,2,1,0:T(1,128)S(1)} %get-tuple-element.21), channel_id=1, source_target_pairs={{1,0},{2,1},{3,2},{0,3},{5,4},{6,5},{7,6},{4,7},{9,8},{10,9},{11,1... | collective-permute-start | bytes 46088 | tf_op jit(solution)/shard_map/ppermute | solution.py:24
  168.6 4.2 %collective-permute-start.18 = (f32[3,1,16,128]{3,2,1,0:T(8,128)S(1)}, f32[3,1,16,128]{3,2,1,0:T(8,128)S(1)}, u32[]{:S(2)}, u32[]{:S(2)}) collective-permute-start(f32[3,1,16,128]{3,2,1,0:T(8,128)S(1)} %get-tuple-element.30), channel_id=1, source_target_pairs={{0,4},{4,8},{8,12},{12,16},{16,20},{20,24},{24,28},{28,0},{1,5},{5... | collective-permute-start | bytes 73736 | tf_op jit(solution)/shard_map/ppermute | solution.py:23
  168.7 4.2 %collective-permute-start.19 = (f32[3,1,16,128]{3,2,1,0:T(8,128)S(1)}, f32[3,1,16,128]{3,2,1,0:T(8,128)S(1)}, u32[]{:S(2)}, u32[]{:S(2)}) collective-permute-start(f32[3,1,16,128]{3,2,1,0:T(8,128)S(1)} %get-tuple-element.31), channel_id=1, source_target_pairs={{4,0},{8,4},{12,8},{16,12},{20,16},{24,20},{28,24},{0,28},{5,1},{9... | collective-permute-start | bytes 73736 | tf_op jit(solution)/shard_map/ppermute | solution.py:24
  172.9 5.6 %collective-permute-start.20 = (f32[3,10,1,128]{3,2,1,0:T(1,128)S(1)}, f32[3,10,1,128]{3,2,1,0:T(1,128)S(1)}, u32[]{:S(2)}, u32[]{:S(2)}) collective-permute-start(f32[3,10,1,128]{3,2,1,0:T(1,128)S(1)} %get-tuple-element.18), channel_id=1, source_target_pairs={{0,1},{1,2},{2,3},{3,0},{4,5},{5,6},{6,7},{7,4},{8,9},{9,10},{10,1... | collective-permute-start | bytes 46088 | tf_op jit(solution)/shard_map/ppermute | solution.py:23
  174.8 3.8 %collective-permute-start.21 = (f32[3,10,1,128]{3,2,1,0:T(1,128)S(1)}, f32[3,10,1,128]{3,2,1,0:T(1,128)S(1)}, u32[]{:S(2)}, u32[]{:S(2)}) collective-permute-start(f32[3,10,1,128]{3,2,1,0:T(1,128)S(1)} %get-tuple-element.19), channel_id=1, source_target_pairs={{1,0},{2,1},{3,2},{0,3},{5,4},{6,5},{7,6},{4,7},{9,8},{10,9},{11,1... | collective-permute-start | bytes 46088 | tf_op jit(solution)/shard_map/ppermute | solution.py:24
  218.9 5.5 %collective-permute-start.23 = (f32[8,1,128]{2,1,0:T(1,128)S(1)}, f32[8,1,128]{2,1,0:T(1,128)S(1)}, u32[]{:S(2)}, u32[]{:S(2)}) collective-permute-start(f32[8,1,128]{2,1,0:T(1,128)S(1)} %slice.610), channel_id=1, source_target_pairs={{0,1},{1,2},{2,3},{3,0},{4,5},{5,6},{6,7},{7,4},{8,9},{9,10},{10,1... | collective-permute-start | bytes 12296 | tf_op jit(solution)/shard_map/ppermute | solution.py:13
  221.0 4.0 %collective-permute-start.22 = (f32[1,16,128]{2,1,0:T(8,128)S(1)}, f32[1,16,128]{2,1,0:T(8,128)S(1)}, u32[]{:S(2)}, u32[]{:S(2)}) collective-permute-start(f32[1,16,128]{2,1,0:T(8,128)S(1)} %slice_bitcast_fusion.6), channel_id=1, source_target_pairs={{0,4},{4,8},{8,12},{12,16},{16,20},{20,24},{24,28},{28,0},{1,5},{5... | collective-permute-start | bytes 24584 | tf_op jit(solution)/shard_map/ppermute | solution.py:13
  225.3 4.0 %collective-permute-start.25 = (f32[1,16,128]{2,1,0:T(8,128)S(1)}, f32[1,16,128]{2,1,0:T(8,128)S(1)}, u32[]{:S(2)}, u32[]{:S(2)}) collective-permute-start(f32[1,16,128]{2,1,0:T(8,128)S(1)} %get-tuple-element.65), channel_id=1, source_target_pairs={{0,4},{4,8},{8,12},{12,16},{16,20},{20,24},{24,28},{28,0},{1,5},{5... | collective-permute-start | bytes 24584 | tf_op jit(solution)/shard_map/ppermute | solution.py:23
  231.1 5.4 %collective-permute-start.27 = (f32[10,1,128]{2,1,0:T(1,128)S(1)}, f32[10,1,128]{2,1,0:T(1,128)S(1)}, u32[]{:S(2)}, u32[]{:S(2)}) collective-permute-start(f32[10,1,128]{2,1,0:T(1,128)S(1)} %get-tuple-element.50), channel_id=1, source_target_pairs={{0,1},{1,2},{2,3},{3,0},{4,5},{5,6},{6,7},{7,4},{8,9},{9,10},{10,1... | collective-permute-start | bytes 15368 | tf_op jit(solution)/shard_map/ppermute | solution.py:23
  236.7 4.0 %collective-permute-start.29 = (f32[1,16,128]{2,1,0:T(8,128)S(1)}, f32[1,16,128]{2,1,0:T(8,128)S(1)}, u32[]{:S(2)}, u32[]{:S(2)}) collective-permute-start(f32[1,16,128]{2,1,0:T(8,128)S(1)} %get-tuple-element.61), channel_id=1, source_target_pairs={{0,4},{4,8},{8,12},{12,16},{16,20},{20,24},{24,28},{28,0},{1,5},{5... | collective-permute-start | bytes 24584 | tf_op jit(solution)/shard_map/ppermute | solution.py:23
  240.8 5.5 %collective-permute-start.31 = (f32[10,1,128]{2,1,0:T(1,128)S(1)}, f32[10,1,128]{2,1,0:T(1,128)S(1)}, u32[]{:S(2)}, u32[]{:S(2)}) collective-permute-start(f32[10,1,128]{2,1,0:T(1,128)S(1)} %get-tuple-element.48), channel_id=1, source_target_pairs={{0,1},{1,2},{2,3},{3,0},{4,5},{5,6},{6,7},{7,4},{8,9},{9,10},{10,1... | collective-permute-start | bytes 15368 | tf_op jit(solution)/shard_map/ppermute | solution.py:23
  256.5 4.0 %collective-permute-start.33 = (f32[1,16,128]{2,1,0:T(8,128)S(1)}, f32[1,16,128]{2,1,0:T(8,128)S(1)}, u32[]{:S(2)}, u32[]{:S(2)}) collective-permute-start(f32[1,16,128]{2,1,0:T(8,128)S(1)} %get-tuple-element.57), channel_id=1, source_target_pairs={{0,4},{4,8},{8,12},{12,16},{16,20},{20,24},{24,28},{28,0},{1,5},{5... | collective-permute-start | bytes 24584 | tf_op jit(solution)/shard_map/ppermute | solution.py:23
  262.5 5.4 %collective-permute-start.35 = (f32[10,1,128]{2,1,0:T(1,128)S(1)}, f32[10,1,128]{2,1,0:T(1,128)S(1)}, u32[]{:S(2)}, u32[]{:S(2)}) collective-permute-start(f32[10,1,128]{2,1,0:T(1,128)S(1)} %get-tuple-element.46), channel_id=1, source_target_pairs={{0,1},{1,2},{2,3},{3,0},{4,5},{5,6},{6,7},{7,4},{8,9},{9,10},{10,1... | collective-permute-start | bytes 15368 | tf_op jit(solution)/shard_map/ppermute | solution.py:23
  268.1 4.0 %collective-permute-start.37 = (f32[1,16,128]{2,1,0:T(8,128)S(1)}, f32[1,16,128]{2,1,0:T(8,128)S(1)}, u32[]{:S(2)}, u32[]{:S(2)}) collective-permute-start(f32[1,16,128]{2,1,0:T(8,128)S(1)} %get-tuple-element.53), channel_id=1, source_target_pairs={{0,4},{4,8},{8,12},{12,16},{16,20},{20,24},{24,28},{28,0},{1,5},{5... | collective-permute-start | bytes 24584 | tf_op jit(solution)/shard_map/ppermute | solution.py:23
  272.2 5.5 %collective-permute-start.39 = (f32[10,1,128]{2,1,0:T(1,128)S(1)}, f32[10,1,128]{2,1,0:T(1,128)S(1)}, u32[]{:S(2)}, u32[]{:S(2)}) collective-permute-start(f32[10,1,128]{2,1,0:T(1,128)S(1)} %get-tuple-element.44), channel_id=1, source_target_pairs={{0,1},{1,2},{2,3},{3,0},{4,5},{5,6},{6,7},{7,4},{8,9},{9,10},{10,1... | collective-permute-start | bytes 15368 | tf_op jit(solution)/shard_map/ppermute | solution.py:23
  (16 other events, 284.3 us)
where the time goes:
time: 279 us; the launch traced here: 278 us
  blocking collectives  167 us (60%)
  waiting for transfers between devices  50.3 us (18%)
  starting transfers between devices  48.6 us (17%)
  local copies, waits for them, and re-layouts  4.57 us (2%)
  other arithmetic  4.35 us (2%)
    psum x4, blocking collectives, global_sums(): return lax.psum(local, ('gx', 'gz'))  159 us
    ppermute x18, waiting for transfers between devices, with_halo(): before = lax.ppermute(last, axis, up)  34.2 us
    ppermute x18, starting transfers between devices, with_halo(): after = lax.ppermute(initial, axis, down)  27.8 us
    ppermute x18, starting transfers between devices, with_halo(): before = lax.ppermute(last, axis, up)  15.6 us
    ppermute x18, waiting for transfers between devices, with_halo(): after = lax.ppermute(initial, axis, down)  9.46 us
    unnamed x1, blocking collectives  8.52 us
    ppermute x4, waiting for transfers between devices, passed_along(): return lax.ppermute(value, axis, pairs)  6.56 us
  transfers between devices with their start and end apart: 40, of which 30 were waited for; matrix products, arithmetic and copies ran while one was open for 1% of the time, Pallas kernels for 0%

commit v1 on v0

--- a/solution.py
+++ b/solution.py
@@ -5,6 +5,11 @@
 
 COARSE = 16
 jacobi_weight = 2.0 / 3.0
+
+
+def summed_here(x, mesh_axis):
+    blocks = lax.all_gather(x, mesh_axis)
+    return jnp.sum(blocks, axis=0)
 
 
 def passed_along(value, axis, steps):
@@ -36,7 +41,7 @@
 
 def global_sums(pairs):
     local = jnp.stack([inner_local(left, right) for left, right in pairs])
-    return lax.psum(local, ("gx", "gz"))
+    return summed_here(local, ("gx", "gz"))
 
 
 def solve_values(velocity_old, source, diag_coef, face_coef):

time: 279 us -> 363 us (1.30)
  blocking collectives: 167 us -> 252 us
    all_gather x0 -> x3, blocking collectives: none -> 204 us  [summed_here(): blocks = lax.all_gather(x, mesh_axis)]
    psum x4 -> x0, blocking collectives: 159 us -> none  [global_sums(): return lax.psum(local, ('gx', 'gz'))]
    unnamed x1 -> x2, blocking collectives: 8.52 us -> 47.6 us
    ppermute x18, starting transfers between devices: 27.8 us -> 32 us  [with_halo(): after = lax.ppermute(initial, axis, down)]
    ppermute x18, starting transfers between devices: 15.6 us -> 11.7 us  [with_halo(): before = lax.ppermute(last, axis, up)]
  transfers between devices with their start and end apart: 40 -> 40, of which waited for: 30 -> 27; matrix products, arithmetic and copies ran while one was open for 1% -> 1% of each run, Pallas kernels for 0% -> 0%
where the time goes in v1:
time: 363 us
  blocking collectives  252 us (69%)
  waiting for transfers between devices  51.5 us (14%)
  starting transfers between devices  46.9 us (13%)
  local copies, waits for them, and re-layouts  4.86 us (1%)
  other arithmetic  4.52 us (1%)
    all_gather x3, blocking collectives, summed_here(): blocks = lax.all_gather(x, mesh_axis)  204 us
    unnamed x2, blocking collectives  47.6 us
    ppermute x18, waiting for transfers between devices, with_halo(): before = lax.ppermute(last, axis, up)  34.8 us
    ppermute x18, starting transfers between devices, with_halo(): after = lax.ppermute(initial, axis, down)  32 us
    ppermute x18, starting transfers between devices, with_halo(): before = lax.ppermute(last, axis, up)  11.7 us
    ppermute x18, waiting for transfers between devices, with_halo(): after = lax.ppermute(initial, axis, down)  8.77 us
    ppermute x4, waiting for transfers between devices, passed_along(): return lax.ppermute(value, axis, pairs)  7.9 us
  transfers between devices with their start and end apart: 40, of which 27 were waited for; matrix products, arithmetic and copies ran while one was open for 1% of the time, Pallas kernels for 0%

profile of v1, /device:TPU:0, one launch (start us, length us, event | category | flops | bytes accessed | tf_op | source)
XLA Modules:
  0.0 362.9 jit_solution(10108983711025950101)
XLA Ops:
  1.6 3.1 collective-permute-start.3
  4.8 2.6 collective-permute-start.2
  9.5 2.6 collective-permute-done
  13.8 2.2 collective-permute-start.5
  18.1 2.6 collective-permute-start.7
  23.9 2.5 collective-permute-start.9
  28.4 68.1 %all-gather.4 = f32[32,2,3]{2,1,0:T(2,128)S(1)} all-gather(f32[1,2,3]{2,1,0:T(2,128)S(1)} %maximum_bitcast_fusion.1), channel_id=2, replica_groups=mesh['gx'=8,'gz'=4] {'gx','gz'}, dimensions={0}, use_global_device_ids=true | all-gather | bytes 792 | tf_op jit(solution)/shard_map/all_gather | solution.py:11
  96.7 2.6 collective-permute-start.11
  101.0 3.8 %collective-permute-start.13 = (f32[3,10,1,128]{3,2,1,0:T(1,128)S(1)}, f32[3,10,1,128]{3,2,1,0:T(1,128)S(1)}, u32[]{:S(2)}, u32[]{:S(2)}) collective-permute-start(f32[3,10,1,128]{3,2,1,0:T(1,128)S(1)} %get-tuple-element.23), channel_id=1, source_target_pairs={{1,0},{2,1},{3,2},{0,3},{5,4},{6,5},{7,6},{4,7},{9,8},{10,9},{11,1... | collective-permute-start | bytes 46088 | tf_op jit(solution)/shard_map/ppermute | solution.py:29
  106.8 68.2 %all-gather.5 = f32[32,4,3]{2,1,0:T(4,128)S(1)} all-gather(f32[1,4,3]{2,1,0:T(4,128)S(1)} %maximum_bitcast_fusion), channel_id=3, replica_groups=mesh['gx'=8,'gz'=4] {'gx','gz'}, dimensions={0}, use_global_device_ids=true | all-gather | bytes 1584 | tf_op jit(solution)/shard_map/all_gather | solution.py:11
  175.3 2.6 collective-permute-start.15
  179.6 3.8 %collective-permute-start.17 = (f32[3,10,1,128]{3,2,1,0:T(1,128)S(1)}, f32[3,10,1,128]{3,2,1,0:T(1,128)S(1)}, u32[]{:S(2)}, u32[]{:S(2)}) collective-permute-start(f32[3,10,1,128]{3,2,1,0:T(1,128)S(1)} %get-tuple-element.21), channel_id=1, source_target_pairs={{1,0},{2,1},{3,2},{0,3},{5,4},{6,5},{7,6},{4,7},{9,8},{10,9},{11,1... | collective-permute-start | bytes 46088 | tf_op jit(solution)/shard_map/ppermute | solution.py:29
  183.4 1.7 collective-permute-done.16
  185.6 39.1 %all-reduce.19 = f32[96]{0:T(128)S(1)} all-reduce(f32[96]{0:T(128)S(1)} %dynamic-update-slice), channel_id=4, replica_groups=mesh['gx'=8,'gz'=4] {'gx','gz'}, use_global_device_ids=true, to_apply=%add.19 | all-reduce | flops 96 | bytes 768
  225.0 2.6 collective-permute-start.19
  229.2 2.2 collective-permute-start.20
  231.4 1.7 collective-permute-start.21
  233.1 1.7 collective-permute-done.20
  235.5 67.7 %all-gather.6 = f32[32,2,3]{2,1,0:T(2,128)S(1)} all-gather(f32[1,2,3]{2,1,0:T(2,128)S(1)} %maximum_bitcast_fusion.2), channel_id=5, replica_groups=mesh['gx'=8,'gz'=4] {'gx','gz'}, dimensions={0}, use_global_device_ids=true | all-gather | bytes 792 | tf_op jit(solution)/shard_map/all_gather | solution.py:11
  303.5 5.3 %collective-permute-done.23 = f32[8,1,128]{2,1,0:T(1,128)S(1)} collective-permute-done((f32[8,1,128]{2,1,0:T(1,128)S(1)}, f32[8,1,128]{2,1,0:T(1,128)S(1)}, u32[]{:S(2)}, u32[]{:S(2)}) %collective-permute-start.23) | collective-permute-done | bytes 4128 | tf_op jit(solution)/shard_map/ppermute | solution.py:18
  310.4 2.7 collective-permute-done.25
  313.1 2.4 collective-permute-start.26
  316.9 4.1 %collective-permute-done.27 = f32[10,1,128]{2,1,0:T(1,128)S(1)} collective-permute-done((f32[10,1,128]{2,1,0:T(1,128)S(1)}, f32[10,1,128]{2,1,0:T(1,128)S(1)}, u32[]{:S(2)}, u32[]{:S(2)}) %collective-permute-start.27) | collective-permute-done | bytes 5152 | tf_op jit(solution)/shard_map/ppermute | solution.py:28
  325.2 2.0 collective-permute-start.31
  328.9 1.9 collective-permute-done.31
  331.9 8.5 %all-reduce.20 = f32[64]{0:T(128)S(1)} all-reduce(f32[64]{0:T(128)S(1)} %convolution_bitcast_fusion), channel_id=6, replica_groups=mesh['gx'=8,'gz'=4] {'gz'}, use_global_device_ids=true, to_apply=%region_13.14.clone | all-reduce | flops 64 | bytes 512
  342.4 2.7 collective-permute-done.33
  345.0 1.9 collective-permute-start.34
  348.7 3.7 %collective-permute-done.35 = f32[10,1,128]{2,1,0:T(1,128)S(1)} collective-permute-done((f32[10,1,128]{2,1,0:T(1,128)S(1)}, f32[10,1,128]{2,1,0:T(1,128)S(1)}, u32[]{:S(2)}, u32[]{:S(2)}) %collective-permute-start.35) | collective-permute-done | bytes 5152 | tf_op jit(solution)/shard_map/ppermute | solution.py:28
  353.9 2.7 collective-permute-done.37
  356.7 2.0 collective-permute-start.39
  360.3 1.9 collective-permute-done.39
  (162 shorter events, 37.7 us)
Async XLA Ops:
  1.6 7.8 %collective-permute-start.3 = (f32[8,1,128]{2,1,0:T(1,128)S(1)}, f32[8,1,128]{2,1,0:T(1,128)S(1)}, u32[]{:S(2)}, u32[]{:S(2)}) collective-permute-start(f32[8,1,128]{2,1,0:T(1,128)S(1)} %slice.567), channel_id=1, source_target_pairs={{0,1},{1,2},{2,3},{3,0},{4,5},{5,6},{6,7},{7,4},{8,9},{9,10},{10,1... | collective-permute-start | bytes 12296 | tf_op jit(solution)/shard_map/ppermute | solution.py:18
  4.7 7.3 %collective-permute-start.1 = (f32[3,1,16,128]{3,2,1,0:T(8,128)S(1)}, f32[3,1,16,128]{3,2,1,0:T(8,128)S(1)}, u32[]{:S(2)}, u32[]{:S(2)}) collective-permute-start(f32[3,1,16,128]{3,2,1,0:T(8,128)S(1)} %get-tuple-element.42), channel_id=1, source_target_pairs={{0,4},{4,8},{8,12},{12,16},{16,20},{20,24},{24,28},{28,0},{1,5},{5... | collective-permute-start | bytes 73736 | tf_op jit(solution)/shard_map/ppermute | solution.py:28
  4.8 7.4 %collective-permute-start.2 = (f32[3,1,16,128]{3,2,1,0:T(8,128)S(1)}, f32[3,1,16,128]{3,2,1,0:T(8,128)S(1)}, u32[]{:S(2)}, u32[]{:S(2)}) collective-permute-start(f32[3,1,16,128]{3,2,1,0:T(8,128)S(1)} %get-tuple-element.41), channel_id=1, source_target_pairs={{4,0},{8,4},{12,8},{16,12},{20,16},{24,20},{28,24},{0,28},{5,1},{9... | collective-permute-start | bytes 73736 | tf_op jit(solution)/shard_map/ppermute | solution.py:29
  8.1 4.0 %collective-permute-start = (f32[1,16,128]{2,1,0:T(8,128)S(1)}, f32[1,16,128]{2,1,0:T(8,128)S(1)}, u32[]{:S(2)}, u32[]{:S(2)}) collective-permute-start(f32[1,16,128]{2,1,0:T(8,128)S(1)} %slice_bitcast_fusion.7), channel_id=1, source_target_pairs={{0,4},{4,8},{8,12},{12,16},{16,20},{20,24},{24,28},{28,0},{1,5},{5... | collective-permute-start | bytes 24584 | tf_op jit(solution)/shard_map/ppermute | solution.py:18
  12.2 5.6 %collective-permute-start.4 = (f32[3,10,1,128]{3,2,1,0:T(1,128)S(1)}, f32[3,10,1,128]{3,2,1,0:T(1,128)S(1)}, u32[]{:S(2)}, u32[]{:S(2)}) collective-permute-start(f32[3,10,1,128]{3,2,1,0:T(1,128)S(1)} %get-tuple-element.26), channel_id=1, source_target_pairs={{0,1},{1,2},{2,3},{3,0},{4,5},{5,6},{6,7},{7,4},{8,9},{9,10},{10,1... | collective-permute-start | bytes 46088 | tf_op jit(solution)/shard_map/ppermute | solution.py:28
  13.8 4.0 %collective-permute-start.5 = (f32[3,10,1,128]{3,2,1,0:T(1,128)S(1)}, f32[3,10,1,128]{3,2,1,0:T(1,128)S(1)}, u32[]{:S(2)}, u32[]{:S(2)}) collective-permute-start(f32[3,10,1,128]{3,2,1,0:T(1,128)S(1)} %get-tuple-element.27), channel_id=1, source_target_pairs={{1,0},{2,1},{3,2},{0,3},{5,4},{6,5},{7,6},{4,7},{9,8},{10,9},{11,1... | collective-permute-start | bytes 46088 | tf_op jit(solution)/shard_map/ppermute | solution.py:29
  18.0 4.4 %collective-permute-start.6 = (f32[3,1,16,128]{3,2,1,0:T(8,128)S(1)}, f32[3,1,16,128]{3,2,1,0:T(8,128)S(1)}, u32[]{:S(2)}, u32[]{:S(2)}) collective-permute-start(f32[3,1,16,128]{3,2,1,0:T(8,128)S(1)} %get-tuple-element.36), channel_id=1, source_target_pairs={{0,4},{4,8},{8,12},{12,16},{16,20},{20,24},{24,28},{28,0},{1,5},{5... | collective-permute-start | bytes 73736 | tf_op jit(solution)/shard_map/ppermute | solution.py:28
  18.1 4.4 %collective-permute-start.7 = (f32[3,1,16,128]{3,2,1,0:T(8,128)S(1)}, f32[3,1,16,128]{3,2,1,0:T(8,128)S(1)}, u32[]{:S(2)}, u32[]{:S(2)}) collective-permute-start(f32[3,1,16,128]{3,2,1,0:T(8,128)S(1)} %get-tuple-element.37), channel_id=1, source_target_pairs={{4,0},{8,4},{12,8},{16,12},{20,16},{24,20},{28,24},{0,28},{5,1},{9... | collective-permute-start | bytes 73736 | tf_op jit(solution)/shard_map/ppermute | solution.py:29
  22.5 5.6 %collective-permute-start.8 = (f32[3,10,1,128]{3,2,1,0:T(1,128)S(1)}, f32[3,10,1,128]{3,2,1,0:T(1,128)S(1)}, u32[]{:S(2)}, u32[]{:S(2)}) collective-permute-start(f32[3,10,1,128]{3,2,1,0:T(1,128)S(1)} %get-tuple-element.24), channel_id=1, source_target_pairs={{0,1},{1,2},{2,3},{3,0},{4,5},{5,6},{6,7},{7,4},{8,9},{9,10},{10,1... | collective-permute-start | bytes 46088 | tf_op jit(solution)/shard_map/ppermute | solution.py:28
  23.9 4.2 %collective-permute-start.9 = (f32[3,10,1,128]{3,2,1,0:T(1,128)S(1)}, f32[3,10,1,128]{3,2,1,0:T(1,128)S(1)}, u32[]{:S(2)}, u32[]{:S(2)}) collective-permute-start(f32[3,10,1,128]{3,2,1,0:T(1,128)S(1)} %get-tuple-element.25), channel_id=1, source_target_pairs={{1,0},{2,1},{3,2},{0,3},{5,4},{6,5},{7,6},{4,7},{9,8},{10,9},{11,1... | collective-permute-start | bytes 46088 | tf_op jit(solution)/shard_map/ppermute | solution.py:29
  96.6 4.2 %collective-permute-start.10 = (f32[3,1,16,128]{3,2,1,0:T(8,128)S(1)}, f32[3,1,16,128]{3,2,1,0:T(8,128)S(1)}, u32[]{:S(2)}, u32[]{:S(2)}) collective-permute-start(f32[3,1,16,128]{3,2,1,0:T(8,128)S(1)} %get-tuple-element.34), channel_id=1, source_target_pairs={{0,4},{4,8},{8,12},{12,16},{16,20},{20,24},{24,28},{28,0},{1,5},{5... | collective-permute-start | bytes 73736 | tf_op jit(solution)/shard_map/ppermute | solution.py:28
  96.7 4.2 %collective-permute-start.11 = (f32[3,1,16,128]{3,2,1,0:T(8,128)S(1)}, f32[3,1,16,128]{3,2,1,0:T(8,128)S(1)}, u32[]{:S(2)}, u32[]{:S(2)}) collective-permute-start(f32[3,1,16,128]{3,2,1,0:T(8,128)S(1)} %get-tuple-element.35), channel_id=1, source_target_pairs={{4,0},{8,4},{12,8},{16,12},{20,16},{24,20},{28,24},{0,28},{5,1},{9... | collective-permute-start | bytes 73736 | tf_op jit(solution)/shard_map/ppermute | solution.py:29
  100.9 5.6 %collective-permute-start.12 = (f32[3,10,1,128]{3,2,1,0:T(1,128)S(1)}, f32[3,10,1,128]{3,2,1,0:T(1,128)S(1)}, u32[]{:S(2)}, u32[]{:S(2)}) collective-permute-start(f32[3,10,1,128]{3,2,1,0:T(1,128)S(1)} %get-tuple-element.22), channel_id=1, source_target_pairs={{0,1},{1,2},{2,3},{3,0},{4,5},{5,6},{6,7},{7,4},{8,9},{9,10},{10,1... | collective-permute-start | bytes 46088 | tf_op jit(solution)/shard_map/ppermute | solution.py:28
  101.0 5.5 %collective-permute-start.13 = (f32[3,10,1,128]{3,2,1,0:T(1,128)S(1)}, f32[3,10,1,128]{3,2,1,0:T(1,128)S(1)}, u32[]{:S(2)}, u32[]{:S(2)}) collective-permute-start(f32[3,10,1,128]{3,2,1,0:T(1,128)S(1)} %get-tuple-element.23), channel_id=1, source_target_pairs={{1,0},{2,1},{3,2},{0,3},{5,4},{6,5},{7,6},{4,7},{9,8},{10,9},{11,1... | collective-permute-start | bytes 46088 | tf_op jit(solution)/shard_map/ppermute | solution.py:29
  175.3 4.2 %collective-permute-start.14 = (f32[3,1,16,128]{3,2,1,0:T(8,128)S(1)}, f32[3,1,16,128]{3,2,1,0:T(8,128)S(1)}, u32[]{:S(2)}, u32[]{:S(2)}) collective-permute-start(f32[3,1,16,128]{3,2,1,0:T(8,128)S(1)} %get-tuple-element.32), channel_id=1, source_target_pairs={{0,4},{4,8},{8,12},{12,16},{16,20},{20,24},{24,28},{28,0},{1,5},{5... | collective-permute-start | bytes 73736 | tf_op jit(solution)/shard_map/ppermute | solution.py:28
  175.3 4.2 %collective-permute-start.15 = (f32[3,1,16,128]{3,2,1,0:T(8,128)S(1)}, f32[3,1,16,128]{3,2,1,0:T(8,128)S(1)}, u32[]{:S(2)}, u32[]{:S(2)}) collective-permute-start(f32[3,1,16,128]{3,2,1,0:T(8,128)S(1)} %get-tuple-element.33), channel_id=1, source_target_pairs={{4,0},{8,4},{12,8},{16,12},{20,16},{24,20},{28,24},{0,28},{5,1},{9... | collective-permute-start | bytes 73736 | tf_op jit(solution)/shard_map/ppermute | solution.py:29
  179.5 5.6 %collective-permute-start.16 = (f32[3,10,1,128]{3,2,1,0:T(1,128)S(1)}, f32[3,10,1,128]{3,2,1,0:T(1,128)S(1)}, u32[]{:S(2)}, u32[]{:S(2)}) collective-permute-start(f32[3,10,1,128]{3,2,1,0:T(1,128)S(1)} %get-tuple-element.20), channel_id=1, source_target_pairs={{0,1},{1,2},{2,3},{3,0},{4,5},{5,6},{6,7},{7,4},{8,9},{9,10},{10,1... | collective-permute-start | bytes 46088 | tf_op jit(solution)/shard_map/ppermute | solution.py:28
  179.6 5.5 %collective-permute-start.17 = (f32[3,10,1,128]{3,2,1,0:T(1,128)S(1)}, f32[3,10,1,128]{3,2,1,0:T(1,128)S(1)}, u32[]{:S(2)}, u32[]{:S(2)}) collective-permute-start(f32[3,10,1,128]{3,2,1,0:T(1,128)S(1)} %get-tuple-element.21), channel_id=1, source_target_pairs={{1,0},{2,1},{3,2},{0,3},{5,4},{6,5},{7,6},{4,7},{9,8},{10,9},{11,1... | collective-permute-start | bytes 46088 | tf_op jit(solution)/shard_map/ppermute | solution.py:29
  225.0 4.2 %collective-permute-start.18 = (f32[3,1,16,128]{3,2,1,0:T(8,128)S(1)}, f32[3,1,16,128]{3,2,1,0:T(8,128)S(1)}, u32[]{:S(2)}, u32[]{:S(2)}) collective-permute-start(f32[3,1,16,128]{3,2,1,0:T(8,128)S(1)} %get-tuple-element.30), channel_id=1, source_target_pairs={{0,4},{4,8},{8,12},{12,16},{16,20},{20,24},{24,28},{28,0},{1,5},{5... | collective-permute-start | bytes 73736 | tf_op jit(solution)/shard_map/ppermute | solution.py:28
  225.0 4.2 %collective-permute-start.19 = (f32[3,1,16,128]{3,2,1,0:T(8,128)S(1)}, f32[3,1,16,128]{3,2,1,0:T(8,128)S(1)}, u32[]{:S(2)}, u32[]{:S(2)}) collective-permute-start(f32[3,1,16,128]{3,2,1,0:T(8,128)S(1)} %get-tuple-element.31), channel_id=1, source_target_pairs={{4,0},{8,4},{12,8},{16,12},{20,16},{24,20},{28,24},{0,28},{5,1},{9... | collective-permute-start | bytes 73736 | tf_op jit(solution)/shard_map/ppermute | solution.py:29
  229.2 5.6 %collective-permute-start.20 = (f32[3,10,1,128]{3,2,1,0:T(1,128)S(1)}, f32[3,10,1,128]{3,2,1,0:T(1,128)S(1)}, u32[]{:S(2)}, u32[]{:S(2)}) collective-permute-start(f32[3,10,1,128]{3,2,1,0:T(1,128)S(1)} %get-tuple-element.18), channel_id=1, source_target_pairs={{0,1},{1,2},{2,3},{3,0},{4,5},{5,6},{6,7},{7,4},{8,9},{9,10},{10,1... | collective-permute-start | bytes 46088 | tf_op jit(solution)/shard_map/ppermute | solution.py:28
  303.4 5.5 %collective-permute-start.23 = (f32[8,1,128]{2,1,0:T(1,128)S(1)}, f32[8,1,128]{2,1,0:T(1,128)S(1)}, u32[]{:S(2)}, u32[]{:S(2)}) collective-permute-start(f32[8,1,128]{2,1,0:T(1,128)S(1)} %slice.610), channel_id=1, source_target_pairs={{0,1},{1,2},{2,3},{3,0},{4,5},{5,6},{6,7},{7,4},{8,9},{9,10},{10,1... | collective-permute-start | bytes 12296 | tf_op jit(solution)/shard_map/ppermute | solution.py:18
  303.4 5.4 %collective-permute-start.22 = (f32[1,16,128]{2,1,0:T(8,128)S(1)}, f32[1,16,128]{2,1,0:T(8,128)S(1)}, u32[]{:S(2)}, u32[]{:S(2)}) collective-permute-start(f32[1,16,128]{2,1,0:T(8,128)S(1)} %slice_bitcast_fusion.6), channel_id=1, source_target_pairs={{0,4},{4,8},{8,12},{12,16},{16,20},{20,24},{24,28},{28,0},{1,5},{5... | collective-permute-start | bytes 24584 | tf_op jit(solution)/shard_map/ppermute | solution.py:18
  309.0 4.0 %collective-permute-start.25 = (f32[1,16,128]{2,1,0:T(8,128)S(1)}, f32[1,16,128]{2,1,0:T(8,128)S(1)}, u32[]{:S(2)}, u32[]{:S(2)}) collective-permute-start(f32[1,16,128]{2,1,0:T(8,128)S(1)} %get-tuple-element.65), channel_id=1, source_target_pairs={{0,4},{4,8},{8,12},{12,16},{16,20},{20,24},{24,28},{28,0},{1,5},{5... | collective-permute-start | bytes 24584 | tf_op jit(solution)/shard_map/ppermute | solution.py:28
  313.1 3.8 %collective-permute-start.26 = (f32[10,1,128]{2,1,0:T(1,128)S(1)}, f32[10,1,128]{2,1,0:T(1,128)S(1)}, u32[]{:S(2)}, u32[]{:S(2)}) collective-permute-start(f32[10,1,128]{2,1,0:T(1,128)S(1)} %get-tuple-element.49), channel_id=1, source_target_pairs={{1,0},{2,1},{3,2},{0,3},{5,4},{6,5},{7,6},{4,7},{9,8},{10,9},{11,1... | collective-permute-start | bytes 15368 | tf_op jit(solution)/shard_map/ppermute | solution.py:29
  315.5 5.4 %collective-permute-start.27 = (f32[10,1,128]{2,1,0:T(1,128)S(1)}, f32[10,1,128]{2,1,0:T(1,128)S(1)}, u32[]{:S(2)}, u32[]{:S(2)}) collective-permute-start(f32[10,1,128]{2,1,0:T(1,128)S(1)} %get-tuple-element.50), channel_id=1, source_target_pairs={{0,1},{1,2},{2,3},{3,0},{4,5},{5,6},{6,7},{7,4},{8,9},{9,10},{10,1... | collective-permute-start | bytes 15368 | tf_op jit(solution)/shard_map/ppermute | solution.py:28
  321.1 4.0 %collective-permute-start.29 = (f32[1,16,128]{2,1,0:T(8,128)S(1)}, f32[1,16,128]{2,1,0:T(8,128)S(1)}, u32[]{:S(2)}, u32[]{:S(2)}) collective-permute-start(f32[1,16,128]{2,1,0:T(8,128)S(1)} %get-tuple-element.61), channel_id=1, source_target_pairs={{0,4},{4,8},{8,12},{12,16},{16,20},{20,24},{24,28},{28,0},{1,5},{5... | collective-permute-start | bytes 24584 | tf_op jit(solution)/shard_map/ppermute | solution.py:28
  325.2 5.5 %collective-permute-start.31 = (f32[10,1,128]{2,1,0:T(1,128)S(1)}, f32[10,1,128]{2,1,0:T(1,128)S(1)}, u32[]{:S(2)}, u32[]{:S(2)}) collective-permute-start(f32[10,1,128]{2,1,0:T(1,128)S(1)} %get-tuple-element.48), channel_id=1, source_target_pairs={{0,1},{1,2},{2,3},{3,0},{4,5},{5,6},{6,7},{7,4},{8,9},{9,10},{10,1... | collective-permute-start | bytes 15368 | tf_op jit(solution)/shard_map/ppermute | solution.py:28
  341.0 4.0 %collective-permute-start.33 = (f32[1,16,128]{2,1,0:T(8,128)S(1)}, f32[1,16,128]{2,1,0:T(8,128)S(1)}, u32[]{:S(2)}, u32[]{:S(2)}) collective-permute-start(f32[1,16,128]{2,1,0:T(8,128)S(1)} %get-tuple-element.57), channel_id=1, source_target_pairs={{0,4},{4,8},{8,12},{12,16},{16,20},{20,24},{24,28},{28,0},{1,5},{5... | collective-permute-start | bytes 24584 | tf_op jit(solution)/shard_map/ppermute | solution.py:28
  347.0 5.4 %collective-permute-start.35 = (f32[10,1,128]{2,1,0:T(1,128)S(1)}, f32[10,1,128]{2,1,0:T(1,128)S(1)}, u32[]{:S(2)}, u32[]{:S(2)}) collective-permute-start(f32[10,1,128]{2,1,0:T(1,128)S(1)} %get-tuple-element.46), channel_id=1, source_target_pairs={{0,1},{1,2},{2,3},{3,0},{4,5},{5,6},{6,7},{7,4},{8,9},{9,10},{10,1... | collective-permute-start | bytes 15368 | tf_op jit(solution)/shard_map/ppermute | solution.py:28
  352.6 4.0 %collective-permute-start.37 = (f32[1,16,128]{2,1,0:T(8,128)S(1)}, f32[1,16,128]{2,1,0:T(8,128)S(1)}, u32[]{:S(2)}, u32[]{:S(2)}) collective-permute-start(f32[1,16,128]{2,1,0:T(8,128)S(1)} %get-tuple-element.53), channel_id=1, source_target_pairs={{0,4},{4,8},{8,12},{12,16},{16,20},{20,24},{24,28},{28,0},{1,5},{5... | collective-permute-start | bytes 24584 | tf_op jit(solution)/shard_map/ppermute | solution.py:28
  356.7 5.5 %collective-permute-start.39 = (f32[10,1,128]{2,1,0:T(1,128)S(1)}, f32[10,1,128]{2,1,0:T(1,128)S(1)}, u32[]{:S(2)}, u32[]{:S(2)}) collective-permute-start(f32[10,1,128]{2,1,0:T(1,128)S(1)} %get-tuple-element.44), channel_id=1, source_target_pairs={{0,1},{1,2},{2,3},{3,0},{4,5},{5,6},{6,7},{7,4},{8,9},{9,10},{10,1... | collective-permute-start | bytes 15368 | tf_op jit(solution)/shard_map/ppermute | solution.py:28
  (16 other events, 368.1 us)
